TPU v7x, 256 devices: a whole 4x4x8 slice. The times are simulated.
256 devices in a mesh: leaf: 32 (over z, x), gx: 2 (over core), gy: 4 (over y).
Axes of the slice: x: 4, y: 4, z: 8, core: 2. Of those that a mesh axis runs over, the one named last changes fastest.
Arguments:
- leaf_rhs: float32 [32, 2, 4, 48, 16, 128], P('leaf', 'gx', 'gy'), may hold values from -6 to 6
- leaf_inv: float32 [32, 2, 4, 48, 128, 128], P('leaf', 'gx', 'gy'), may hold values from -0.4 to 1.7
- edge_blocks: float32 [32, 2, 4, 48, 2, 128, 128], P('leaf', 'gx', 'gy'), may hold values from -0.09375 to 0.09375
- edge_target: int32 [32, 2, 4, 48, 2], P('leaf', 'gx', 'gy'), may hold values from 0 to 639
- sep_rhs: float32 [32, 2, 4, 4, 16, 128], P('leaf', 'gx', 'gy'), may hold values from -6 to 6
- sep_inv: float32 [32, 2, 4, 4, 128, 128], P('leaf', 'gx', 'gy'), may hold values from -0.4 to 1.7
- sep_up: float32 [32, 2, 4, 4, 128, 128], P('leaf', 'gx', 'gy'), may hold values from -0.4375 to 0.4375
- sep_parent: int32 [32, 2, 4, 4], P('leaf', 'gx', 'gy'), may hold values from 0 to 3
Outputs:
- leaf_solution: float32 [32, 2, 4, 48, 16, 128], P('leaf', 'gx', 'gy')
- sep_solution: float32 [32, 2, 4, 4, 16, 128], P('leaf', 'gx', 'gy')
All inputs are finite; a program needn't handle non-finite values.
Results may differ from a plain program's by a relative error of at most 0.0003.
Values sent between devices are 32-bit elements; how exact they have to be, the bound alone decides.
No kernel may reach another device: no remote copies, remote signals or barrier semaphores. Data moves between devices by JAX's collectives and lax.ppermute only.
A program may use at most 64 MiB of HBM per device.

v0:
```python
import jax
import jax.numpy as jnp
from jax import lax
from jax.sharding import PartitionSpec as P

HIGHEST = lax.Precision.HIGHEST


def from_behind(value, axis, steps):
    count = lax.axis_size(axis)
    initial, last = (max(0, -steps), min(count, count - steps))
    return lax.ppermute(value, axis, [(source, source + steps) for source in range(initial, last)])


def extended(block, sides, width):
    for axis, dim in sides:
        count = lax.axis_size(axis)
        forward = [(i, i + 1) for i in range(count - 1)]
        backward = [(target, source) for source, target in forward]
        low = lax.ppermute(
            lax.slice_in_dim(block, block.shape[dim] - width, None, axis=dim), axis, forward
        )
        high = lax.ppermute(lax.slice_in_dim(block, 0, width, axis=dim), axis, backward)
        block = jnp.concatenate([low, block, high], axis=dim)
    return block


def along_rows(value, offset):
    return from_behind(value, "gx", offset)


def along_cols(value, offset):
    return from_behind(value, "gy", offset)


def along_levels(value, offset):
    return from_behind(value, "leaf", offset)


def local(leaf_rhs, leaf_inv, edge_blocks, edge_target, sep_rhs, sep_inv, sep_up, sep_parent):
    levels = lax.axis_size("leaf")
    rhs_leaf = leaf_rhs[0, 0, 0]
    inv_leaf = leaf_inv[0, 0, 0]
    blocks = edge_blocks[0, 0, 0]
    target = edge_target[0, 0, 0]
    rhs_sep = sep_rhs[0, 0, 0]
    inv_sep = sep_inv[0, 0, 0]
    up_blocks = sep_up[0, 0, 0]
    parent = sep_parent[0, 0, 0]
    slot_count, rhs_cols, block_width = rhs_leaf.shape
    sep_count = rhs_sep.shape[0]
    targets = 5 * levels * sep_count
    leaf_mid = jnp.einsum("srw,svw->srv", rhs_leaf, inv_leaf, precision=HIGHEST)
    products = jnp.einsum("srw,skvw->skrv", leaf_mid, blocks, precision=HIGHEST)
    chosen = (target[:, :, None] == jnp.arange(targets, dtype=jnp.int32)).astype(jnp.float32)
    outgoing = jnp.einsum("skt,skrv->trv", chosen, products, precision=HIGHEST)
    outgoing = outgoing.reshape(5, levels, sep_count, rhs_cols, block_width)
    arriving = outgoing[0] + along_rows(outgoing[2], 1) + along_rows(outgoing[1], -1)
    arriving = arriving + along_cols(outgoing[4], 1) + along_cols(outgoing[3], -1)
    updates = lax.psum_scatter(arriving, "leaf", scatter_dimension=0, tiled=True)[0]
    reduced = rhs_sep - updates
    parent_pick = (parent[:, None] == jnp.arange(sep_count, dtype=jnp.int32)).astype(jnp.float32)

    def solve_up(incoming):
        partial_mid = jnp.einsum("srw,svw->srv", reduced - incoming, inv_sep, precision=HIGHEST)
        lifted = jnp.einsum("crw,cvw->crv", partial_mid, up_blocks, precision=HIGHEST)
        return (partial_mid, jnp.einsum("cp,crv->prv", parent_pick, lifted, precision=HIGHEST))

    def solve_down(sep_mid, from_above):
        parents = jnp.einsum("cp,prw->crw", parent_pick, from_above, precision=HIGHEST)
        pushed = jnp.einsum("crv,cvw->crw", parents, up_blocks, precision=HIGHEST)
        return jnp.einsum("srv,svw->srw", sep_mid - pushed, inv_sep, precision=HIGHEST)

    empty = jnp.zeros_like(rhs_sep)

    def forward_step(turn, incoming):
        return along_levels(solve_up(incoming)[1], 1)

    incoming = lax.fori_loop(0, levels - 1, forward_step, empty)
    sep_mid = solve_up(incoming)[0]

    def backward_step(turn, from_above):
        return along_levels(solve_down(sep_mid, from_above), -1)

    from_above = lax.fori_loop(0, levels - 1, backward_step, empty)
    sep_sol = solve_down(sep_mid, from_above)
    every_level = lax.all_gather(sep_sol[None], "leaf", axis=0, tiled=True)
    padded = extended(every_level[None, None], (("gx", 0), ("gy", 1)), 1)
    solved_table = jnp.stack([padded[1, 1], padded[0, 1], padded[2, 1], padded[1, 0], padded[1, 2]])
    solved_table = solved_table.reshape(targets, rhs_cols * block_width)
    reached = jnp.dot(chosen.reshape(-1, targets), solved_table, precision=HIGHEST)
    reached = reached.reshape(slot_count, -1, rhs_cols, block_width)
    pulled_back = jnp.einsum("skrv,skvw->srw", reached, blocks, precision=HIGHEST)
    leaf_sol = jnp.einsum("srv,svw->srw", leaf_mid - pulled_back, inv_leaf, precision=HIGHEST)
    return (leaf_sol[None, None, None], sep_sol[None, None, None])


def solution(mesh):
    in_specs = (
        P("leaf", "gx", "gy", None, None, None),
        P("leaf", "gx", "gy", None, None, None),
        P("leaf", "gx", "gy", None, None, None, None),
        P("leaf", "gx", "gy", None, None),
        P("leaf", "gx", "gy", None, None, None),
        P("leaf", "gx", "gy", None, None, None),
        P("leaf", "gx", "gy", None, None, None),
        P("leaf", "gx", "gy", None),
    )
    out_specs = (P("leaf", "gx", "gy", None, None, None), P("leaf", "gx", "gy", None, None, None))
    return jax.shard_map(local, mesh=mesh, in_specs=in_specs, out_specs=out_specs, check_vma=False)
```

profile of v0, /device:TPU:1, one launch (start us, length us, event | category | flops | bytes accessed | tf_op | source)
XLA Modules:
  0.0 1161.4 jit_solution(9223311347620786621)
XLA Ops:
  9.1 6.0 fusion.22
  15.0 7.4 fusion.24
  40.8 10.1 collective-permute-done.5
  54.5 219.2 %reduce-scatter.2.cloned.1.call-done = f32[1,4,16,128]{3,2,1,0:T(8,128)} async-done(((f32[32,4,16,128]{3,2,1,0:T(8,128)}), f32[1,4,16,128]{3,2,1,0:T(8,128)}) %reduce-scatter.2.cloned.1.call-update) | async-done | bytes 32784 | tf_op jit(solution)/shard_map/reduce_scatter | solution.py:60
  274.6 267.6 %while.22 = (s32[]{:T(128)}, f32[4,16,128]{2,0,1:T(4,128)S(1)}, f32[4,16,128]{2,0,1:T(4,128)S(1)}, f32[4,128,128]{2,1,0:T(8,128)S(1)}, f32[4,128,128]{2,1,0:T(8,128)}, /*index=5*/s32[4]{0:T(128)S(1)}, s32[]{:T(128)}) while((s32[]{:T(128)}, f32[4,16,128]{2,0,1:T(4,128)S(1)}, f32[4,16,128]{2,0,1:T(4,128)S(1)}, ...), condition=%wide.region_2.0_spmd.clone, body=%wide.region_1.0_spmd.clone.sunk | while | flops 25567264 | bytes 950405 | solution.py:79
  318.8 5.8 collective-permute-start
  327.8 5.9 collective-permute-start
  345.9 5.8 collective-permute-start
  354.9 5.8 collective-permute-start
  390.8 5.8 collective-permute-start
  399.8 5.9 collective-permute-start
  408.9 6.1 collective-permute-start
  445.1 5.8 collective-permute-start
  463.1 5.8 collective-permute-start
  472.1 5.8 collective-permute-start
  481.0 5.9 collective-permute-start
  490.2 6.1 collective-permute-start
  499.5 5.8 collective-permute-start
  535.4 5.8 collective-permute-start
  542.6 296.4 %while.23 = (s32[]{:T(128)}, f32[4,16,128]{2,1,0:T(8,128)S(1)}, f32[4,128,128]{2,1,0:T(8,128)}, f32[4,16,128]{2,1,0:T(8,128)S(1)}, f32[4,128,128]{2,1,0:T(8,128)S(1)}, /*index=5*/s32[4]{0:T(128)S(1)}, s32[]{:T(128)}) while((s32[]{:T(128)}, f32[4,16,128]{2,1,0:T(8,128)S(1)}, f32[4,128,128]{2,1,0:T(8,128)}, ...), condition=%wide.region_4.0_spmd.clone, body=%wide.region_3.0_spmd.clone.sunk | while | flops 25567264 | bytes 884869 | solution.py:85
  563.7 5.9 collective-permute-done.1
  572.8 6.1 collective-permute-done.1
  625.2 5.9 collective-permute-done.1
  634.3 6.1 collective-permute-done.1
  643.5 7.0 collective-permute-done.1
  653.6 6.8 collective-permute-done.1
  663.6 7.4 collective-permute-done.1
  674.2 6.7 collective-permute-done.1
  684.0 7.3 collective-permute-done.1
  694.5 6.9 collective-permute-done.1
  704.5 6.4 collective-permute-done.1
  714.1 6.3 collective-permute-done.1
  723.6 6.5 collective-permute-done.1
  733.2 7.2 collective-permute-done.1
  743.6 6.1 collective-permute-done.1
  752.9 6.8 collective-permute-done.1
  762.9 7.1 collective-permute-done.1
  773.2 6.4 collective-permute-done.1
  782.8 7.0 collective-permute-done.1
  793.0 6.8 collective-permute-done.1
  802.9 6.3 collective-permute-done.1
  812.4 6.7 collective-permute-done.1
  822.3 7.2 collective-permute-done.1
  832.7 6.4 collective-permute-done.1
  841.5 200.2 %all-gather.3.cloned.1.call-done = f32[128,16,128]{2,1,0:T(8,128)} async-done(((f32[4,16,128]{2,1,0:T(8,128)}), f32[128,16,128]{2,1,0:T(8,128)}) %all-gather.3.cloned.1.call-update) | async-done | bytes 1048592 | tf_op jit(solution)/shard_map/all_gather | solution.py:87
  1043.2 7.8 collective-permute-start.7
  1059.8 65.3 %collective-permute-done.8 = f32[3,1,32,4,16,128]{5,4,3,2,1,0:T(8,128)S(1)} collective-permute-done((f32[3,1,32,4,16,128]{5,4,3,2,1,0:T(8,128)S(1)}, f32[3,1,32,4,16,128]{5,4,3,2,1,0:T(8,128)S(1)}, u32[]{:S(2)}, u32[]{:S(2)}) %collective-permute-start.8) | collective-permute-done | bytes 3145760 | tf_op jit(solution)/shard_map/ppermute | solution.py:20
  1134.1 6.0 copy.59
  (361 shorter events, 382.6 us)
Async XLA Ops:
  7.2 266.6 %reduce-scatter.2.cloned.1.call-start = ((), (), s32[]{:S(2)}) async-start(), calls=%async_computation.1 | async-start | bytes 1081344 | tf_op jit(solution)/shard_map/reduce_scatter | solution.py:60
  26.2 24.7 %collective-permute-start.5 = (f32[32,4,16,128]{3,2,1,0:T(8,128)S(1)}, f32[32,4,16,128]{3,2,1,0:T(8,128)S(1)}, u32[]{:S(2)}, u32[]{:S(2)}) collective-permute-start(f32[32,4,16,128]{3,2,1,0:T(8,128)S(1)} %copy.53), channel_id=1, source_target_pairs={{1,0},{2,1},{3,2},{5,4},{6,5},{7,6},{9,8},{10,9},{11,10},{13,12},{... | collective-permute-start | bytes 3145736 | tf_op jit(solution)/shard_map/ppermute | solution.py:12
  28.2 24.3 %collective-permute-start.4 = (f32[32,4,16,128]{3,2,1,0:T(8,128)S(1)}, f32[32,4,16,128]{3,2,1,0:T(8,128)S(1)}, u32[]{:S(2)}, u32[]{:S(2)}) collective-permute-start(f32[32,4,16,128]{3,2,1,0:T(8,128)S(1)} %copy.52), channel_id=1, source_target_pairs={{0,1},{1,2},{2,3},{4,5},{5,6},{6,7},{8,9},{9,10},{10,11},{12,13},{... | collective-permute-start | bytes 3145736 | tf_op jit(solution)/shard_map/ppermute | solution.py:12
  33.5 19.0 %collective-permute-start.3 = (f32[32,4,16,128]{3,2,1,0:T(8,128)S(1)}, f32[32,4,16,128]{3,2,1,0:T(8,128)S(1)}, u32[]{:S(2)}, u32[]{:S(2)}) collective-permute-start(f32[32,4,16,128]{3,2,1,0:T(8,128)S(1)} %copy.51), channel_id=1, source_target_pairs={{4,0},{5,1},{6,2},{7,3},{12,8},{13,9},{14,10},{15,11},{20,16},{21,... | collective-permute-start | bytes 3145736 | tf_op jit(solution)/shard_map/ppermute | solution.py:12
  39.4 13.1 %collective-permute-start.2 = (f32[32,4,16,128]{3,2,1,0:T(8,128)S(1)}, f32[32,4,16,128]{3,2,1,0:T(8,128)S(1)}, u32[]{:S(2)}, u32[]{:S(2)}) collective-permute-start(f32[32,4,16,128]{3,2,1,0:T(8,128)S(1)} %copy.49), channel_id=1, source_target_pairs={{0,4},{1,5},{2,6},{3,7},{8,12},{9,13},{10,14},{11,15},{16,20},{17,... | collective-permute-start | bytes 3145736 | tf_op jit(solution)/shard_map/ppermute | solution.py:12
  54.5 987.3 %all-gather.3.cloned.1.call-start = ((), (), s32[]{:S(2)}) async-start(), calls=%async_computation.2 | async-start | bytes 1081344 | tf_op jit(solution)/shard_map/all_gather | solution.py:87
  318.8 6.8 collective-permute-start
  327.8 6.9 collective-permute-start
  345.9 6.8 collective-permute-start
  354.9 6.8 collective-permute-start
  390.8 6.8 collective-permute-start
  399.8 7.0 collective-permute-start
  408.9 7.1 collective-permute-start
  445.1 6.8 collective-permute-start
  463.1 6.8 collective-permute-start
  481.0 7.0 collective-permute-start
  490.2 7.1 collective-permute-start
  535.4 6.8 collective-permute-start
  544.5 7.0 collective-permute-start.1
  553.4 7.1 collective-permute-start.1
  562.4 7.2 collective-permute-start.1
  571.5 7.4 collective-permute-start.1
  623.9 7.2 collective-permute-start.1
  633.0 7.4 collective-permute-start.1
  642.2 8.3 collective-permute-start.1
  652.3 8.1 collective-permute-start.1
  662.3 8.7 collective-permute-start.1
  672.9 8.0 collective-permute-start.1
  682.7 8.6 collective-permute-start.1
  693.2 8.2 collective-permute-start.1
  703.2 7.7 collective-permute-start.1
  712.8 7.6 collective-permute-start.1
  722.3 7.8 collective-permute-start.1
  731.9 8.5 collective-permute-start.1
  742.3 7.4 collective-permute-start.1
  751.6 8.1 collective-permute-start.1
  761.6 8.4 collective-permute-start.1
  771.9 7.7 collective-permute-start.1
  781.5 8.3 collective-permute-start.1
  791.7 8.1 collective-permute-start.1
  801.6 7.6 collective-permute-start.1
  811.1 8.0 collective-permute-start.1
  821.0 8.5 collective-permute-start.1
  831.4 7.7 collective-permute-start.1
  1041.8 9.5 collective-permute-start.6
  1043.2 10.2 collective-permute-start.7
  1055.0 70.2 %collective-permute-start.8 = (f32[3,1,32,4,16,128]{5,4,3,2,1,0:T(8,128)S(1)}, f32[3,1,32,4,16,128]{5,4,3,2,1,0:T(8,128)S(1)}, u32[]{:S(2)}, u32[]{:S(2)}) collective-permute-start(f32[3,1,32,4,16,128]{5,4,3,2,1,0:T(8,128)S(1)} %pad_maximum_fusion), channel_id=1, source_target_pairs={{0,1},{1,2},{2,3},{4,5},{5,6},{6,7},{8,9},{9,10},{10,11},{12,13},{... | collective-permute-start | bytes 9437192 | tf_op jit(solution)/shard_map/ppermute | solution.py:20
  1058.3 70.9 %collective-permute-start.9 = (f32[3,1,32,4,16,128]{5,4,3,2,1,0:T(8,128)S(1)}, f32[3,1,32,4,16,128]{5,4,3,2,1,0:T(8,128)S(1)}, u32[]{:S(2)}, u32[]{:S(2)}) collective-permute-start(f32[3,1,32,4,16,128]{5,4,3,2,1,0:T(8,128)S(1)} %pad_maximum_fusion), channel_id=1, source_target_pairs={{1,0},{2,1},{3,2},{5,4},{6,5},{7,6},{9,8},{10,9},{11,10},{13,12},{... | collective-permute-start | bytes 9437192 | tf_op jit(solution)/shard_map/ppermute | solution.py:23
  (32 other events, 920.9 us)
Sparse Core Ops, SparseCore 0:
  54.6 219.0 reduce-scatter.1
  841.7 200.0 all-gather.2
where the time goes:
time: 1170 us; the launch traced here: 1160 us
  waiting for transfers between devices  732 us (63%)
  starting transfers between devices  234 us (20%)
  matrix products  159 us (14%)
  local copies, waits for them, and re-layouts  16.1 us (1%)
  between operations  14.3 us (1%)
    ppermute x66, waiting for transfers between devices, from_behind(): lax.ppermute(value, axis, [(source, source + steps) for source in range(i...  241 us
    ppermute x66, starting transfers between devices, from_behind(): lax.ppermute(value, axis, [(source, source + steps) for source in range(i...  220 us
    reduce_scatter x1, waiting for transfers between devices, local(): lax.psum_scatter(arriving, 'leaf', scatter_dimension=0, tiled=True)[0]  219 us
    all_gather x1, waiting for transfers between devices, local(): every_level = lax.all_gather(sep_sol[None], 'leaf', axis=0, tiled=True)  200 us
    ppermute x2, waiting for transfers between devices, extended(): lax.ppermute(lax.slice_in_dim(block, block.shape[dim] - width, None, axis...  65.6 us
    dot_general x31, matrix products, solve_up(): jnp.einsum('crw,cvw->crv', partial_mid, up_blocks, precision=HIGHEST)  45.6 us
    dot_general x32, matrix products, solve_down(): pushed = jnp.einsum('crv,cvw->crw', parents, up_blocks, precision=HIGHEST)  40.8 us
  transfers between devices with their start and end apart: 72, of which 70 were waited for; matrix products, arithmetic and copies ran while one was open for 0% of the time, Pallas kernels for 0%

commit v1 on v0

--- a/solution.py
+++ b/solution.py
@@ -2,6 +2,7 @@
 import jax.numpy as jnp
 from jax import lax
 from jax.sharding import PartitionSpec as P
+from jax.lax import all_to_all, psum
 
 HIGHEST = lax.Precision.HIGHEST
 
@@ -84,7 +85,9 @@
 
     from_above = lax.fori_loop(0, levels - 1, backward_step, empty)
     sep_sol = solve_down(sep_mid, from_above)
-    every_level = lax.all_gather(sep_sol[None], "leaf", axis=0, tiled=True)
+    every_level = jnp.concatenate(
+        all_to_all(jnp.stack([sep_sol[None]] * psum(1, "leaf"), axis=0), "leaf", 0, 0), axis=0
+    )
     padded = extended(every_level[None, None], (("gx", 0), ("gy", 1)), 1)
     solved_table = jnp.stack([padded[1, 1], padded[0, 1], padded[2, 1], padded[1, 0], padded[1, 2]])
     solved_table = solved_table.reshape(targets, rhs_cols * block_width)

time: 1170 us -> 1120 us (0.957)
  waiting for transfers between devices: 732 us -> 532 us
  blocking collectives: 0 us -> 78.4 us
  starting transfers between devices: 234 us -> 307 us
    all_gather x1 -> x0, waiting for transfers between devices: 200 us -> none  [local(): every_level = lax.all_gather(sep_sol[None], 'leaf', axis=0, tiled=True)]
    all_to_all x0 -> x1, blocking collectives: none -> 78.4 us  [local(): all_to_all(jnp.stack([sep_sol[None]] * psum(1, 'leaf'), axis=0), 'leaf',...]
    ppermute x2, starting transfers between devices: 9.05 us -> 82.2 us  [extended(): lax.ppermute(lax.slice_in_dim(block, 0, width, axis=dim), axis, backward)]
  transfers between devices with their start and end apart: 72 -> 71, of which waited for: 70 -> 69; matrix products, arithmetic and copies ran while one was open for 0% -> 0% of each run, Pallas kernels for 0% -> 0%
where the time goes in v1:
time: 1120 us; the launch traced here: 1110 us
  waiting for transfers between devices  532 us (48%)
  starting transfers between devices  307 us (27%)
  matrix products  158 us (14%)
  blocking collectives  78.4 us (7%)
  local copies, waits for them, and re-layouts  16.2 us (1%)
  between operations  14.3 us (1%)
    ppermute x66, waiting for transfers between devices, from_behind(): lax.ppermute(value, axis, [(source, source + steps) for source in range(i...  241 us
    ppermute x66, starting transfers between devices, from_behind(): lax.ppermute(value, axis, [(source, source + steps) for source in range(i...  220 us
    reduce_scatter x1, waiting for transfers between devices, local(): lax.psum_scatter(arriving, 'leaf', scatter_dimension=0, tiled=True)[0]  219 us
    ppermute x2, starting transfers between devices, extended(): lax.ppermute(lax.slice_in_dim(block, 0, width, axis=dim), axis, backward)  82.2 us
    all_to_all x1, blocking collectives, local(): all_to_all(jnp.stack([sep_sol[None]] * psum(1, 'leaf'), axis=0), 'leaf',...  78.4 us
    ppermute x2, waiting for transfers between devices, extended(): lax.ppermute(lax.slice_in_dim(block, block.shape[dim] - width, None, axis...  65.4 us
    dot_general x31, matrix products, solve_up(): jnp.einsum('crw,cvw->crv', partial_mid, up_blocks, precision=HIGHEST)  45.6 us
    dot_general x32, matrix products, solve_down(): pushed = jnp.einsum('crv,cvw->crw', parents, up_blocks, precision=HIGHEST)  40.8 us
  transfers between devices with their start and end apart: 71, of which 69 were waited for; matrix products, arithmetic and copies ran while one was open for 0% of the time, Pallas kernels for 0%

profile of v1, /device:TPU:1, one launch (start us, length us, event | category | flops | bytes accessed | tf_op | source)
XLA Modules:
  0.0 1110.7 jit_solution(15617150365513127179)
XLA Ops:
  9.1 6.0 fusion.22
  15.0 7.4 fusion.24
  40.8 10.1 collective-permute-done.5
  54.5 219.3 %reduce-scatter.2.cloned.1.call-done = f32[1,4,16,128]{3,2,1,0:T(8,128)} async-done(((f32[32,4,16,128]{3,2,1,0:T(8,128)}), f32[1,4,16,128]{3,2,1,0:T(8,128)}) %reduce-scatter.2.cloned.1.call-update) | async-done | bytes 32784 | tf_op jit(solution)/shard_map/reduce_scatter | solution.py:61
  274.6 267.6 %while.22 = (s32[]{:T(128)}, f32[4,16,128]{2,0,1:T(4,128)S(1)}, f32[4,16,128]{2,0,1:T(4,128)S(1)}, f32[4,128,128]{2,1,0:T(8,128)S(1)}, f32[4,128,128]{2,1,0:T(8,128)}, /*index=5*/s32[4]{0:T(128)S(1)}, s32[]{:T(128)}) while((s32[]{:T(128)}, f32[4,16,128]{2,0,1:T(4,128)S(1)}, f32[4,16,128]{2,0,1:T(4,128)S(1)}, ...), condition=%wide.region_2.0_spmd.clone, body=%wide.region_1.0_spmd.clone.sunk | while | flops 25567264 | bytes 950405 | solution.py:80
  309.9 5.8 collective-permute-start
  318.8 5.8 collective-permute-start
  327.8 5.9 collective-permute-start
  345.9 5.8 collective-permute-start
  363.9 5.8 collective-permute-start
  381.8 5.8 collective-permute-start
  390.8 5.8 collective-permute-start
  399.8 5.9 collective-permute-start
  408.9 6.1 collective-permute-start
  418.2 5.8 collective-permute-start
  454.1 5.8 collective-permute-start
  472.0 5.8 collective-permute-start
  481.0 5.9 collective-permute-start
  490.2 6.1 collective-permute-start
  526.4 5.8 collective-permute-start
  542.6 296.4 %while.23 = (s32[]{:T(128)}, f32[4,16,128]{2,1,0:T(8,128)S(1)}, f32[4,128,128]{2,1,0:T(8,128)}, f32[4,16,128]{2,1,0:T(8,128)S(1)}, f32[4,128,128]{2,1,0:T(8,128)S(1)}, /*index=5*/s32[4]{0:T(128)S(1)}, s32[]{:T(128)}) while((s32[]{:T(128)}, f32[4,16,128]{2,1,0:T(8,128)S(1)}, f32[4,128,128]{2,1,0:T(8,128)}, ...), condition=%wide.region_4.0_spmd.clone, body=%wide.region_3.0_spmd.clone.sunk | while | flops 25567264 | bytes 884869 | solution.py:86
  563.7 5.9 collective-permute-done.1
  572.8 6.1 collective-permute-done.1
  625.2 5.9 collective-permute-done.1
  643.2 7.3 collective-permute-done.1
  653.7 6.7 collective-permute-done.1
  663.6 7.4 collective-permute-done.1
  674.2 6.7 collective-permute-done.1
  684.0 7.3 collective-permute-done.1
  694.5 6.4 collective-permute-done.1
  704.0 6.9 collective-permute-done.1
  714.1 6.3 collective-permute-done.1
  723.6 6.5 collective-permute-done.1
  733.2 7.2 collective-permute-done.1
  743.6 6.1 collective-permute-done.1
  752.9 6.9 collective-permute-done.1
  762.9 7.1 collective-permute-done.1
  773.2 6.4 collective-permute-done.1
  782.7 7.0 collective-permute-done.1
  792.9 6.8 collective-permute-done.1
  803.0 6.3 collective-permute-done.1
  812.4 6.7 collective-permute-done.1
  822.2 7.2 collective-permute-done.1
  832.6 6.4 collective-permute-done.1
  841.0 78.4 %all_to_all.5 = f32[32,1,4,16,128]{4,3,2,1,0:T(8,128)S(1)} all-to-all(f32[32,1,4,16,128]{4,3,2,1,0:T(8,128)S(1)} %stack.6), channel_id=1, replica_groups=mesh['leaf'=32,'gx'=2,'gy'=4] {'leaf'}, dimensions={0} | all-to-all | bytes 2097152 | tf_op jit(solution)/shard_map/all_to_all | solution.py:89
  920.7 80.9 %collective-permute-start.7 = (f32[1,1,32,4,16,128]{5,4,3,2,1,0:T(8,128)S(1)}, f32[1,1,32,4,16,128]{5,4,3,2,1,0:T(8,128)S(1)}, u32[]{:S(2)}, u32[]{:S(2)}) collective-permute-start(f32[1,1,32,4,16,128]{5,4,3,2,1,0:T(8,128)S(1)} %bitcast.139), channel_id=1, source_target_pairs={{4,0},{5,1},{6,2},{7,3},{12,8},{13,9},{14,10},{15,11},{20,16},{21,... | collective-permute-start | bytes 3145736 | tf_op jit(solution)/shard_map/ppermute | solution.py:24
  1009.1 65.3 %collective-permute-done.8 = f32[3,1,32,4,16,128]{5,4,3,2,1,0:T(8,128)S(1)} collective-permute-done((f32[3,1,32,4,16,128]{5,4,3,2,1,0:T(8,128)S(1)}, f32[3,1,32,4,16,128]{5,4,3,2,1,0:T(8,128)S(1)}, u32[]{:S(2)}, u32[]{:S(2)}) %collective-permute-start.8) | collective-permute-done | bytes 3145760 | tf_op jit(solution)/shard_map/ppermute | solution.py:21
  1083.3 6.0 copy.80
  (360 shorter events, 380.4 us)
Async XLA Ops:
  7.2 266.6 %reduce-scatter.2.cloned.1.call-start = ((), (), s32[]{:S(2)}) async-start(), calls=%async_computation.2 | async-start | bytes 1081344 | tf_op jit(solution)/shard_map/reduce_scatter | solution.py:61
  26.2 24.7 %collective-permute-start.5 = (f32[32,4,16,128]{3,2,1,0:T(8,128)S(1)}, f32[32,4,16,128]{3,2,1,0:T(8,128)S(1)}, u32[]{:S(2)}, u32[]{:S(2)}) collective-permute-start(f32[32,4,16,128]{3,2,1,0:T(8,128)S(1)} %copy.74), channel_id=1, source_target_pairs={{1,0},{2,1},{3,2},{5,4},{6,5},{7,6},{9,8},{10,9},{11,10},{13,12},{... | collective-permute-start | bytes 3145736 | tf_op jit(solution)/shard_map/ppermute | solution.py:13
  28.2 24.3 %collective-permute-start.4 = (f32[32,4,16,128]{3,2,1,0:T(8,128)S(1)}, f32[32,4,16,128]{3,2,1,0:T(8,128)S(1)}, u32[]{:S(2)}, u32[]{:S(2)}) collective-permute-start(f32[32,4,16,128]{3,2,1,0:T(8,128)S(1)} %copy.73), channel_id=1, source_target_pairs={{0,1},{1,2},{2,3},{4,5},{5,6},{6,7},{8,9},{9,10},{10,11},{12,13},{... | collective-permute-start | bytes 3145736 | tf_op jit(solution)/shard_map/ppermute | solution.py:13
  33.5 19.0 %collective-permute-start.3 = (f32[32,4,16,128]{3,2,1,0:T(8,128)S(1)}, f32[32,4,16,128]{3,2,1,0:T(8,128)S(1)}, u32[]{:S(2)}, u32[]{:S(2)}) collective-permute-start(f32[32,4,16,128]{3,2,1,0:T(8,128)S(1)} %copy.72), channel_id=1, source_target_pairs={{4,0},{5,1},{6,2},{7,3},{12,8},{13,9},{14,10},{15,11},{20,16},{21,... | collective-permute-start | bytes 3145736 | tf_op jit(solution)/shard_map/ppermute | solution.py:13
  39.4 13.1 %collective-permute-start.2 = (f32[32,4,16,128]{3,2,1,0:T(8,128)S(1)}, f32[32,4,16,128]{3,2,1,0:T(8,128)S(1)}, u32[]{:S(2)}, u32[]{:S(2)}) collective-permute-start(f32[32,4,16,128]{3,2,1,0:T(8,128)S(1)} %copy.70), channel_id=1, source_target_pairs={{0,4},{1,5},{2,6},{3,7},{8,12},{9,13},{10,14},{11,15},{16,20},{17,... | collective-permute-start | bytes 3145736 | tf_op jit(solution)/shard_map/ppermute | solution.py:13
  309.9 6.8 collective-permute-start
  318.8 6.8 collective-permute-start
  327.8 6.9 collective-permute-start
  363.9 6.8 collective-permute-start
  381.8 6.8 collective-permute-start
  390.8 6.8 collective-permute-start
  399.8 7.0 collective-permute-start
  408.9 7.1 collective-permute-start
  454.1 6.8 collective-permute-start
  472.0 6.8 collective-permute-start
  481.0 7.0 collective-permute-start
  490.2 7.1 collective-permute-start
  526.4 6.8 collective-permute-start
  544.5 7.1 collective-permute-start.1
  553.5 7.1 collective-permute-start.1
  562.4 7.2 collective-permute-start.1
  571.5 7.4 collective-permute-start.1
  623.9 7.2 collective-permute-start.1
  633.0 7.0 collective-permute-start.1
  641.9 8.6 collective-permute-start.1
  652.4 8.0 collective-permute-start.1
  662.3 8.7 collective-permute-start.1
  672.9 8.0 collective-permute-start.1
  682.7 8.6 collective-permute-start.1
  693.2 7.7 collective-permute-start.1
  702.7 8.2 collective-permute-start.1
  712.8 7.6 collective-permute-start.1
  722.3 7.8 collective-permute-start.1
  731.9 8.5 collective-permute-start.1
  742.3 7.4 collective-permute-start.1
  751.6 8.2 collective-permute-start.1
  761.6 8.4 collective-permute-start.1
  771.9 7.7 collective-permute-start.1
  781.4 8.3 collective-permute-start.1
  791.6 8.1 collective-permute-start.1
  801.7 7.6 collective-permute-start.1
  811.1 8.0 collective-permute-start.1
  820.9 8.5 collective-permute-start.1
  831.3 7.7 collective-permute-start.1
  919.4 82.3 %collective-permute-start.6 = (f32[1,1,32,4,16,128]{5,4,3,2,1,0:T(8,128)S(1)}, f32[1,1,32,4,16,128]{5,4,3,2,1,0:T(8,128)S(1)}, u32[]{:S(2)}, u32[]{:S(2)}) collective-permute-start(f32[1,1,32,4,16,128]{5,4,3,2,1,0:T(8,128)S(1)} %bitcast.138), channel_id=1, source_target_pairs={{0,4},{1,5},{2,6},{3,7},{8,12},{9,13},{10,14},{11,15},{16,20},{17,... | collective-permute-start | bytes 3145736 | tf_op jit(solution)/shard_map/ppermute | solution.py:21
  920.7 83.1 %collective-permute-start.7 = (f32[1,1,32,4,16,128]{5,4,3,2,1,0:T(8,128)S(1)}, f32[1,1,32,4,16,128]{5,4,3,2,1,0:T(8,128)S(1)}, u32[]{:S(2)}, u32[]{:S(2)}) collective-permute-start(f32[1,1,32,4,16,128]{5,4,3,2,1,0:T(8,128)S(1)} %bitcast.139), channel_id=1, source_target_pairs={{4,0},{5,1},{6,2},{7,3},{12,8},{13,9},{14,10},{15,11},{20,16},{21,... | collective-permute-start | bytes 3145736 | tf_op jit(solution)/shard_map/ppermute | solution.py:24
  1004.2 70.2 %collective-permute-start.8 = (f32[3,1,32,4,16,128]{5,4,3,2,1,0:T(8,128)S(1)}, f32[3,1,32,4,16,128]{5,4,3,2,1,0:T(8,128)S(1)}, u32[]{:S(2)}, u32[]{:S(2)}) collective-permute-start(f32[3,1,32,4,16,128]{5,4,3,2,1,0:T(8,128)S(1)} %pad_maximum_fusion), channel_id=1, source_target_pairs={{0,1},{1,2},{2,3},{4,5},{5,6},{6,7},{8,9},{9,10},{10,11},{12,13},{... | collective-permute-start | bytes 9437192 | tf_op jit(solution)/shard_map/ppermute | solution.py:21
  1007.6 70.9 %collective-permute-start.9 = (f32[3,1,32,4,16,128]{5,4,3,2,1,0:T(8,128)S(1)}, f32[3,1,32,4,16,128]{5,4,3,2,1,0:T(8,128)S(1)}, u32[]{:S(2)}, u32[]{:S(2)}) collective-permute-start(f32[3,1,32,4,16,128]{5,4,3,2,1,0:T(8,128)S(1)} %pad_maximum_fusion), channel_id=1, source_target_pairs={{1,0},{2,1},{3,2},{5,4},{6,5},{7,6},{9,8},{10,9},{11,10},{13,12},{... | collective-permute-start | bytes 9437192 | tf_op jit(solution)/shard_map/ppermute | solution.py:24
  (31 other events, 1064.3 us)
Sparse Core Ops, SparseCore 0:
  54.6 219.0 reduce-scatter.1
